TPU v7x, 32 devices: a whole 2x2x4 slice. The times are simulated.
32 devices in a mesh: dev: 32 (over z, y, x, core).
Axes of the slice: x: 2, y: 2, z: 4, core: 2. Of those that a mesh axis runs over, the one named last changes fastest.
Arguments:
- tokens: bfloat16 [32768, 384], P('dev'), may hold values from -6 to 6
- image_ids: int32 [32768], replicated, may hold values from 0 to 220, never falling along the last dimension, each value on 1 to 197 neighbouring positions
- cotangent: bfloat16 [32768, 384], P('dev'), may hold values from -6 to 6
- w_qkv: bfloat16 [2, 384, 1152], P(None, 'dev'), may hold values from -0.3125 to 0.3125
- bias_qv: bfloat16 [2, 768], P(None, 'dev'), may hold values from -3 to 3
- w_out: bfloat16 [2, 384, 384], P(None, 'dev'), may hold values from -1.25 to 1.25
- bias_out: bfloat16 [2, 384], P(None, 'dev'), may hold values from -3 to 3
- w_up: bfloat16 [2, 384, 1536], P(None, 'dev'), may hold values from -0.3125 to 0.3125
- bias_up: bfloat16 [2, 1536], P(None, 'dev'), may hold values from -3 to 3
- w_down: bfloat16 [2, 1536, 384], P(None, 'dev'), may hold values from -0.15625 to 0.15625
- bias_down: bfloat16 [2, 384], P(None, 'dev'), may hold values from -3 to 3
- norm1_gain: bfloat16 [2, 384], P(None, 'dev'), may hold values from 0.5 to 1.5
- norm1_shift: bfloat16 [2, 384], P(None, 'dev'), may hold values from -1.75 to 1.75
- norm2_gain: bfloat16 [2, 384], P(None, 'dev'), may hold values from 0.5 to 1.5
- norm2_shift: bfloat16 [2, 384], P(None, 'dev'), may hold values from -1.75 to 1.75
Outputs:
- output: bfloat16 [32768, 384], P('dev')
- grad_tokens: float32 [32768, 384], P('dev')
- grad_w_qkv: float32 [2, 384, 1152], P(None, 'dev')
- grad_bias_qv: float32 [2, 768], P(None, 'dev')
- grad_w_out: float32 [2, 384, 384], P(None, 'dev')
- grad_bias_out: float32 [2, 384], P(None, 'dev')
- grad_w_up: float32 [2, 384, 1536], P(None, 'dev')
- grad_bias_up: float32 [2, 1536], P(None, 'dev')
- grad_w_down: float32 [2, 1536, 384], P(None, 'dev')
- grad_bias_down: float32 [2, 384], P(None, 'dev')
- grad_norm1_gain: float32 [2, 384], P(None, 'dev')
- grad_norm1_shift: float32 [2, 384], P(None, 'dev')
- grad_norm2_gain: float32 [2, 384], P(None, 'dev')
- grad_norm2_shift: float32 [2, 384], P(None, 'dev')
Inputs may be any that keep to these rules, and one draw needn't show every extreme that they name: `image_ids`: image ids never fall along the tokens, so each image is a run of consecutive tokens; every image holds 1 to 197 tokens and one holds exactly 197.
All inputs are finite; a program needn't handle non-finite values.
Results may differ from a plain program's by a relative error of at most 0.012.
Values may be sent and summed in bfloat16 or wider, within the bound.
No kernel may reach another device: no remote copies, remote signals or barrier semaphores. Data moves between devices by JAX's collectives and lax.ppermute only.
A program may use at most 192 MiB of HBM per device.

v0:
```python
import jax
import jax.numpy as jnp
from jax import lax
from jax.sharding import PartitionSpec as P

HEADS = 6
HEAD_DIM = 64
LAYERS = 2
HALO = 256
QB = 512
SCALE = 0.125
NEGATIVE = -1e30
EPSILON = 1e-06


def passed_along(value, axis, steps):
    count = lax.axis_size(axis)
    leading, last = (max(0, -steps), min(count, count - steps))
    return lax.ppermute(value, axis, [(source, source + steps) for source in range(leading, last)])


def padded(block, sides, width):
    for axis, dim in sides:
        count = lax.axis_size(axis)
        forward = [(i, i + 1) for i in range(count - 1)]
        backward = [(target, source) for source, target in forward]
        low = lax.ppermute(
            lax.slice_in_dim(block, block.shape[dim] - width, None, axis=dim), axis, forward
        )
        high = lax.ppermute(lax.slice_in_dim(block, 0, width, axis=dim), axis, backward)
        block = jnp.concatenate([low, block, high], axis=dim)
    return block


def layer_norm(values, gain, shift):
    centre = jnp.mean(values, axis=-1, keepdims=True)
    centred = values - centre
    spread = jnp.mean(centred * centred, axis=-1, keepdims=True)
    return centred * lax.rsqrt(spread + EPSILON) * gain + shift


def product(left, right):
    return jnp.dot(left, right, preferred_element_type=jnp.float32)


def contract_rows(left, right):
    return lax.dot_general(
        left, right, (((0,), (0,)), ((), ())), preferred_element_type=jnp.float32
    )


def contract_last(left, right):
    return lax.dot_general(
        left, right, (((1,), (1,)), ((), ())), preferred_element_type=jnp.float32
    )


def gelu_exact(values):
    return jax.nn.gelu(values, approximate=False)


def fetch_forward(shards):
    return (
        lax.all_gather(shards[0], "dev", axis=0, tiled=True),
        lax.all_gather(shards[1], "dev", axis=0, tiled=True),
        lax.all_gather(shards[2], "dev", axis=0, tiled=True),
        lax.all_gather(shards[3], "dev", axis=0, tiled=True),
        lax.all_gather(shards[4], "dev", axis=0, tiled=True),
        lax.all_gather(shards[5], "dev", axis=0, tiled=True),
        lax.all_gather(shards[6], "dev", axis=0, tiled=True),
        lax.all_gather(shards[7], "dev", axis=0, tiled=True),
        lax.all_gather(shards[8], "dev", axis=0, tiled=True),
        lax.all_gather(shards[9], "dev", axis=0, tiled=True),
        lax.all_gather(shards[10], "dev", axis=0, tiled=True),
        lax.all_gather(shards[11], "dev", axis=0, tiled=True),
    )


def fetch_backward(shards):
    return (
        lax.all_gather(shards[0], "dev", axis=0, tiled=True),
        lax.all_gather(shards[1], "dev", axis=0, tiled=True),
        lax.all_gather(shards[2], "dev", axis=0, tiled=True),
        lax.all_gather(shards[3], "dev", axis=0, tiled=True),
        lax.all_gather(shards[4], "dev", axis=0, tiled=True),
        lax.all_gather(shards[5], "dev", axis=0, tiled=True),
        lax.all_gather(shards[6], "dev", axis=0, tiled=True),
        lax.all_gather(shards[7], "dev", axis=0, tiled=True),
        lax.all_gather(shards[8], "dev", axis=0, tiled=True),
        lax.all_gather(shards[9], "dev", axis=0, tiled=True),
        lax.all_gather(shards[10], "dev", axis=0, tiled=True),
        lax.all_gather(shards[11], "dev", axis=0, tiled=True),
    )


def reduce_layer(terms):
    return (
        lax.psum_scatter(terms[0], "dev", scatter_dimension=0, tiled=True),
        lax.psum_scatter(terms[1], "dev", scatter_dimension=0, tiled=True),
        lax.psum_scatter(terms[2], "dev", scatter_dimension=0, tiled=True),
        lax.psum_scatter(terms[3], "dev", scatter_dimension=0, tiled=True),
        lax.psum_scatter(terms[4], "dev", scatter_dimension=0, tiled=True),
        lax.psum_scatter(terms[5], "dev", scatter_dimension=0, tiled=True),
        lax.psum_scatter(terms[6], "dev", scatter_dimension=0, tiled=True),
        lax.psum_scatter(terms[7], "dev", scatter_dimension=0, tiled=True),
        lax.psum_scatter(terms[8], "dev", scatter_dimension=0, tiled=True),
        lax.psum_scatter(terms[9], "dev", scatter_dimension=0, tiled=True),
        lax.psum_scatter(terms[10], "dev", scatter_dimension=0, tiled=True),
        lax.psum_scatter(terms[11], "dev", scatter_dimension=0, tiled=True),
    )


def block_scores(queries, keys_values, id_query, id_keys, first):
    width = queries.shape[1]
    window = QB + 2 * HALO
    query_block = lax.dynamic_slice_in_dim(queries, first, QB, 0).reshape(QB, HEADS, HEAD_DIM)
    key_window = lax.dynamic_slice_in_dim(keys_values, first, window, 0)
    key_heads = key_window[:, :width].reshape(window, HEADS, HEAD_DIM)
    value_heads = key_window[:, width:].reshape(window, HEADS, HEAD_DIM)
    query_ids = lax.dynamic_slice_in_dim(id_query, first, QB, 0)
    window_ids = lax.dynamic_slice_in_dim(id_keys, first, window, 0)
    same_image = query_ids[:, None] == window_ids[None, :]
    scores = (
        jnp.einsum("qhd,khd->hqk", query_block, key_heads, preferred_element_type=jnp.float32)
        * SCALE
    )
    scores = jnp.where(same_image[None], scores, NEGATIVE)
    return (query_block, key_heads, value_heads, scores)


def attend(queries, keys_values, id_query, id_keys):
    row_count, width = queries.shape

    def one_block(block_no):
        first = block_no * QB
        query_block, key_heads, value_heads, scores = block_scores(
            queries, keys_values, id_query, id_keys, first
        )
        highest = jnp.max(scores, axis=2, keepdims=True)
        exponent_terms = jnp.exp(scores - highest)
        totals = jnp.sum(exponent_terms, axis=2, keepdims=True)
        soft_low = (exponent_terms / totals).astype(jnp.bfloat16)
        attended = jnp.einsum(
            "hqk,khd->qhd", soft_low, value_heads, preferred_element_type=jnp.float32
        )
        return (
            attended.reshape(QB, width).astype(jnp.bfloat16),
            (highest + jnp.log(totals))[:, :, 0],
        )

    attended, log_totals = lax.map(one_block, jnp.arange(row_count // QB, dtype=jnp.int32))
    return (attended.reshape(row_count, width), log_totals)


def attend_back(queries, keys_values, id_query, id_keys, log_totals, grad_attended):
    row_count, width = queries.shape
    window = QB + 2 * HALO

    def one_block(block_no, carry):
        grad_queries, grad_window = carry
        first = block_no * QB
        query_block, key_heads, value_heads, scores = block_scores(
            queries, keys_values, id_query, id_keys, first
        )
        soft = jnp.exp(scores - log_totals[block_no][:, :, None])
        grad_block = lax.dynamic_slice_in_dim(grad_attended, first, QB, 0).reshape(
            QB, HEADS, HEAD_DIM
        )
        grad_soft = jnp.einsum(
            "qhd,khd->hqk", grad_block, value_heads, preferred_element_type=jnp.float32
        )
        inner = jnp.sum(soft * grad_soft, axis=2, keepdims=True)
        grad_scores = (soft * (grad_soft - inner)).astype(jnp.bfloat16)
        block_queries = (
            jnp.einsum(
                "hqk,khd->qhd", grad_scores, key_heads, preferred_element_type=jnp.float32
            ).reshape(QB, width)
            * SCALE
        )
        block_keys = (
            jnp.einsum(
                "hqk,qhd->khd", grad_scores, query_block, preferred_element_type=jnp.float32
            ).reshape(window, width)
            * SCALE
        )
        block_values = jnp.einsum(
            "hqk,qhd->khd",
            soft.astype(jnp.bfloat16),
            grad_block,
            preferred_element_type=jnp.float32,
        ).reshape(window, width)
        grad_queries = lax.dynamic_update_slice_in_dim(grad_queries, block_queries, first, 0)
        previous = lax.dynamic_slice_in_dim(grad_window, first, window, 0)
        grad_window = lax.dynamic_update_slice_in_dim(
            grad_window, previous + jnp.concatenate([block_keys, block_values], axis=1), first, 0
        )
        return (grad_queries, grad_window)

    start_carry = (
        jnp.zeros((row_count, width), jnp.float32),
        jnp.zeros((row_count + 2 * HALO, 2 * width), jnp.float32),
    )
    grad_queries, grad_window = lax.fori_loop(0, row_count // QB, one_block, start_carry)
    from_next = passed_along(grad_window[:HALO].astype(jnp.bfloat16), "dev", -1).astype(jnp.float32)
    from_prior = passed_along(
        grad_window[row_count + HALO :].astype(jnp.bfloat16), "dev", 1
    ).astype(jnp.float32)
    grad_own = grad_window[HALO : HALO + row_count]
    grad_own = grad_own.at[row_count - HALO :].add(from_next)
    grad_own = grad_own.at[:HALO].add(from_prior)
    return (grad_queries, grad_own)


def forward_layer(stream, weights_full, id_query, id_keys):
    (
        w_qkv,
        bias_qv,
        w_out,
        bias_out,
        w_up,
        bias_up,
        w_down,
        bias_down,
        gain_one,
        shift_one,
        gain_two,
        shift_two,
    ) = weights_full
    width = stream.shape[1]
    normed = layer_norm(stream, gain_one.astype(jnp.float32), shift_one.astype(jnp.float32)).astype(
        jnp.bfloat16
    )
    mixed = product(normed, w_qkv)
    bias_float = bias_qv.astype(jnp.float32)
    queries = (mixed[:, :width] + bias_float[:width]).astype(jnp.bfloat16)
    keys_values = jnp.concatenate(
        [mixed[:, width : 2 * width], mixed[:, 2 * width :] + bias_float[width:]], axis=1
    ).astype(jnp.bfloat16)
    rim_keys = padded(keys_values, (("dev", 0),), HALO)
    attended, log_totals = attend(queries, rim_keys, id_query, id_keys)
    after = stream + product(attended, w_out) + bias_out.astype(jnp.float32)
    normed_two = layer_norm(
        after, gain_two.astype(jnp.float32), shift_two.astype(jnp.float32)
    ).astype(jnp.bfloat16)
    pre_hidden = product(normed_two, w_up) + bias_up.astype(jnp.float32)
    hidden = gelu_exact(pre_hidden).astype(jnp.bfloat16)
    result = after + product(hidden, w_down) + bias_down.astype(jnp.float32)
    saved = (
        stream,
        normed,
        queries,
        rim_keys,
        attended,
        log_totals,
        after,
        normed_two,
        pre_hidden,
        hidden,
    )
    return (result, saved)


def backward_layer(grad_stream, saved, weights_full, id_query, id_keys):
    (
        stream,
        normed,
        queries,
        rim_keys,
        attended,
        log_totals,
        after,
        normed_two,
        pre_hidden,
        hidden,
    ) = saved
    (
        w_qkv,
        bias_qv,
        w_out,
        bias_out,
        w_up,
        bias_up,
        w_down,
        bias_down,
        gain_one,
        shift_one,
        gain_two,
        shift_two,
    ) = weights_full
    width = stream.shape[1]
    grad_branch = grad_stream.astype(jnp.bfloat16)
    grad_w_down = contract_rows(hidden, grad_branch)
    grad_bias_down = jnp.sum(grad_branch.astype(jnp.float32), axis=0)
    grad_hidden = contract_last(grad_branch, w_down)
    unused_gelu, gelu_pull = jax.vjp(gelu_exact, pre_hidden)
    grad_pre = gelu_pull(grad_hidden)[0].astype(jnp.bfloat16)
    grad_w_up = contract_rows(normed_two, grad_pre)
    grad_bias_up = jnp.sum(grad_pre.astype(jnp.float32), axis=0)
    grad_normed_two = contract_last(grad_pre, w_up)
    unused_two, norm_two_pull = jax.vjp(
        layer_norm, after, gain_two.astype(jnp.float32), shift_two.astype(jnp.float32)
    )
    grad_norm_after, grad_gain_two, grad_shift_two = norm_two_pull(grad_normed_two)
    grad_after = grad_stream + grad_norm_after
    grad_out_branch = grad_after.astype(jnp.bfloat16)
    grad_w_out = contract_rows(attended, grad_out_branch)
    grad_bias_out = jnp.sum(grad_out_branch.astype(jnp.float32), axis=0)
    grad_attended = contract_last(grad_out_branch, w_out).astype(jnp.bfloat16)
    grad_queries, grad_keys_values = attend_back(
        queries, rim_keys, id_query, id_keys, log_totals, grad_attended
    )
    grad_mixed = jnp.concatenate([grad_queries, grad_keys_values], axis=1).astype(jnp.bfloat16)
    grad_w_qkv = contract_rows(normed, grad_mixed)
    mixed_sums = jnp.sum(grad_mixed.astype(jnp.float32), axis=0)
    grad_bias_qv = jnp.concatenate([mixed_sums[:width], mixed_sums[2 * width :]])
    grad_normed = contract_last(grad_mixed, w_qkv)
    unused_one, norm_one_pull = jax.vjp(
        layer_norm, stream, gain_one.astype(jnp.float32), shift_one.astype(jnp.float32)
    )
    grad_norm_stream, grad_gain_one, grad_shift_one = norm_one_pull(grad_normed)
    gradients = (
        grad_w_qkv,
        grad_bias_qv,
        grad_w_out,
        grad_bias_out,
        grad_w_up,
        grad_bias_up,
        grad_w_down,
        grad_bias_down,
        grad_gain_one,
        grad_shift_one,
        grad_gain_two,
        grad_shift_two,
    )
    return (grad_after + grad_norm_stream, gradients)


def on_device(
    tokens,
    image_ids,
    cotangent,
    w_qkv,
    bias_qv,
    w_out,
    bias_out,
    w_up,
    bias_up,
    w_down,
    bias_down,
    norm1_gain,
    norm1_shift,
    norm2_gain,
    norm2_shift,
):
    row_count = tokens.shape[0]
    first_row = lax.axis_index("dev") * row_count
    rim_ids = jnp.full((HALO,), -1, jnp.int32)
    padded_ids = jnp.concatenate([rim_ids, image_ids, rim_ids])
    id_query = lax.dynamic_slice_in_dim(image_ids, first_row, row_count, 0)
    id_keys = lax.dynamic_slice_in_dim(padded_ids, first_row, row_count + 2 * HALO, 0)
    shards = (
        w_qkv,
        bias_qv,
        w_out,
        bias_out,
        w_up,
        bias_up,
        w_down,
        bias_down,
        norm1_gain,
        norm1_shift,
        norm2_gain,
        norm2_shift,
    )
    stream = tokens.astype(jnp.float32)
    saved_all = []
    weights_all = []
    for layer_no in range(LAYERS):
        weights_full = fetch_forward(tuple((piece[layer_no] for piece in shards)))
        stream, saved = forward_layer(stream, weights_full, id_query, id_keys)
        saved_all.append(saved)
        weights_all.append(weights_full)
    final = stream.astype(jnp.bfloat16)
    grad_stream = cotangent.astype(jnp.float32)
    layer_terms = [None] * LAYERS
    for layer_no in range(LAYERS - 1, -1, -1):
        weights_full = fetch_backward(tuple((piece[layer_no] for piece in shards)))
        grad_stream, gradients = backward_layer(
            grad_stream, saved_all[layer_no], weights_full, id_query, id_keys
        )
        layer_terms[layer_no] = reduce_layer(gradients)
    owned = tuple(
        (
            jnp.stack([layer_terms[layer_no][member] for layer_no in range(LAYERS)])
            for member in range(12)
        )
    )
    return (
        final,
        grad_stream,
        owned[0],
        owned[1],
        owned[2],
        owned[3],
        owned[4],
        owned[5],
        owned[6],
        owned[7],
        owned[8],
        owned[9],
        owned[10],
        owned[11],
    )


def solution(mesh):
    in_specs = (
        P("dev", None),
        P(),
        P("dev", None),
        P(None, "dev", None),
        P(None, "dev"),
        P(None, "dev", None),
        P(None, "dev"),
        P(None, "dev", None),
        P(None, "dev"),
        P(None, "dev", None),
        P(None, "dev"),
        P(None, "dev"),
        P(None, "dev"),
        P(None, "dev"),
        P(None, "dev"),
    )
    out_specs = (
        P("dev", None),
        P("dev", None),
        P(None, "dev", None),
        P(None, "dev"),
        P(None, "dev", None),
        P(None, "dev"),
        P(None, "dev", None),
        P(None, "dev"),
        P(None, "dev", None),
        P(None, "dev"),
        P(None, "dev"),
        P(None, "dev"),
        P(None, "dev"),
        P(None, "dev"),
    )
    return jax.shard_map(
        on_device, mesh=mesh, in_specs=in_specs, out_specs=out_specs, check_vma=False
    )
```

profile of v0, /device:TPU:4, one launch (start us, length us, event | category | flops | bytes accessed | tf_op | source)
XLA Modules:
  0.0 997.2 jit_solution(3221153237229773106)
XLA Ops:
  21.5 42.1 %all-reduce.45 = (bf16[768]{0:T(1024)(128)(2,1)S(1)}, bf16[768]{0:T(1024)(128)(2,1)S(1)}, bf16[384]{0:T(512)(128)(2,1)S(1)}, bf16[384]{0:T(512)(128)(2,1)S(1)}, ...) all-reduce(bf16[768]{0:T(1024)(128)(2,1)S(1)} %dynamic-update-slice, ...), channel_id=5, replica_groups=mesh['dev'=32] {'dev'}, use_global_device_ids=true, to_apply=%add.2 | all-reduce | flops 9216 | bytes 36864
  64.6 41.3 %all-gather.2 = bf16[1,384,1152]{2,0,1:T(2,128)(2,1)S(1)} all-gather(bf16[1,12,1152]{2,0,1:T(2,128)(2,1)S(1)} %get-tuple-element.782), channel_id=4, replica_groups=mesh['dev'=32] {'dev'}, dimensions={1}, use_global_device_ids=true | all-gather | bytes 912384 | tf_op jit(solution)/shard_map/all_gather | solution.py:64
  120.4 41.0 %all-gather.4 = bf16[1,384,384]{2,0,1:T(2,128)(2,1)} all-gather(bf16[1,12,384]{2,0,1:T(2,128)(2,1)S(1)} %get-tuple-element.784), channel_id=6, replica_groups=mesh['dev'=32] {'dev'}, dimensions={1}, use_global_device_ids=true | all-gather | bytes 304128 | tf_op jit(solution)/shard_map/all_gather | solution.py:66
  162.6 46.1 %all-gather.14 = bf16[1,384,1152]{2,0,1:T(2,128)(2,1)} all-gather(bf16[1,12,1152]{2,0,1:T(2,128)(2,1)S(1)} %get-tuple-element.781), channel_id=16, replica_groups=mesh['dev'=32] {'dev'}, dimensions={1}, use_global_device_ids=true | all-gather | bytes 912384 | tf_op jit(solution)/shard_map/all_gather | solution.py:64
  216.6 34.5 %while.58 = (s32[]{:T(128)}, bf16[2,512,384]{2,1,0:T(8,128)(2,1)}, f32[2,6,512]{2,1,0:T(8,128)}, s32[2]{0:T(128)}, bf16[1536,768]{0,1:T(8,128)(2,1)S(1)}, /*inde...) while((s32[]{:T(128)}, bf16[2,512,384]{2,1,0:T(8,128)(2,1)}, ...), condition=%wide.region_5.6_spmd, body=%wide.region_2.5_spmd.sunk | while | flops 843772928 | bytes 47831304 | solution.py:151
  226.3 5.0 fusion.237
  243.5 5.0 fusion.237
  255.4 31.3 %multiply_convert_fusion.3 = (bf16[1024,1536]{1,0:T(8,128)(2,1)}, f32[1024,1536]{1,0:T(8,128)}, f32[1024,1536]{1,0:T(8,128)}) fusion(f32[1536]{0:T(1024)S(1)} %copy-done.112, bf16[1,384,1536]{2,0,1:T(2,128)(2,1)} %all-gather.29.cloned.1.call-done, f32[1024,384]{0,1:T(8,128)} %copy-done.11, f32[384]{0:T(512)S(1)} %copy-done.122, ...), kind=kOutput, calls=%fused_computation.85 | convolution fusion | flops 1313734656 | bytes 18498560 | tf_op jit(solution)/shard_map/dot_general | solution.py:43
  286.7 4.3 fusion.139
  296.8 5.6 collective-permute-start.3
  306.1 39.2 %all-gather.16 = bf16[1,384,384]{2,0,1:T(2,128)(2,1)} all-gather(bf16[1,12,384]{2,0,1:T(2,128)(2,1)S(1)} %copy-done.77), channel_id=18, replica_groups=mesh['dev'=32] {'dev'}, dimensions={1}, use_global_device_ids=true | all-gather | bytes 304128 | tf_op jit(solution)/shard_map/all_gather | solution.py:66
  353.2 32.5 %while.59 = (s32[]{:T(128)}, bf16[2,512,384]{2,1,0:T(8,128)(2,1)}, f32[2,6,512]{2,1,0:T(8,128)}, s32[2]{0:T(128)}, bf16[1536,768]{0,1:T(8,128)(2,1)S(1)}, /*inde...) while((s32[]{:T(128)}, bf16[2,512,384]{2,1,0:T(8,128)(2,1)}, ...), condition=%wide.region_13.14_spmd, body=%wide.region_10.13_spmd.sunk | while | flops 843772928 | bytes 47831304 | solution.py:151
  361.8 5.0 fusion.243
  378.1 5.0 fusion.243
  389.6 20.0 %multiply_convert_fusion.2 = (bf16[1024,1536]{1,0:T(8,128)(2,1)}, f32[1024,1536]{1,0:T(8,128)}, f32[1024,1536]{1,0:T(8,128)}) fusion(f32[1536]{0:T(1024)S(1)} %copy-done.114, bf16[1,384,1536]{2,0,1:T(2,128)(2,1)} %all-gather.33.cloned.1.call-done, f32[1024,384]{0,1:T(8,128)} %copy-done.14, f32[384]{0:T(512)S(1)} %copy-done.126, ...), kind=kOutput, calls=%fused_computation.72 | convolution fusion | flops 1313734656 | bytes 18498560 | tf_op jit(solution)/shard_map/dot_general | solution.py:43
  409.6 9.5 convert_reduce_fusion
  439.2 63.3 %while.60 = (s32[]{:T(128)}, bf16[1024,384]{0,1:T(8,128)(2,1)}, f32[1536,768]{0,1:T(8,128)}, bf16[1536,768]{0,1:T(8,128)(2,1)S(1)}, s32[1024]{0:T(1024)S(1)}, /*...) while((s32[]{:T(128)}, bf16[1024,384]{0,1:T(8,128)(2,1)}, ...), condition=%wide.region_20.21_spmd, body=%wide.region_18.20_spmd.sunk | while | flops 2063332352 | bytes 165468752 | solution.py:203
  450.2 7.1 multiply_reduce_fusion.13
  457.3 6.9 multiply_convert_fusion.6
  481.5 7.1 multiply_reduce_fusion.13
  488.7 6.9 multiply_convert_fusion.6
  506.1 5.7 collective-permute-start.4
  537.6 8.1 convert_reduce_fusion.1
  559.4 61.0 %while.61 = (s32[]{:T(128)}, bf16[1024,384]{0,1:T(8,128)(2,1)}, f32[1536,768]{0,1:T(8,128)}, bf16[1536,768]{0,1:T(8,128)(2,1)S(1)}, s32[1024]{0:T(1024)S(1)}, /*...) while((s32[]{:T(128)}, bf16[1024,384]{0,1:T(8,128)(2,1)}, ...), condition=%wide.region_27.28_spmd, body=%wide.region_25.27_spmd.sunk | while | flops 2063332352 | bytes 165468752 | solution.py:203
  569.3 7.2 multiply_reduce_fusion.14
  576.5 6.9 multiply_convert_fusion.7
  599.6 7.1 multiply_reduce_fusion.14
  606.8 6.9 multiply_convert_fusion.7
  635.0 5.0 fusion.119
  660.7 145.1 %fusion.121 = (f32[16,1152]{1,0:T(8,128)S(1)}, f32[16,1152]{1,0:T(8,128)S(1)}, f32[16,384]{1,0:T(8,128)S(1)}, f32[16,384]{1,0:T(8,128)S(1)}, f32[16,1536]{1,0:T(8,128)S(1)}, /*index=5*/f32[16,1536]{1,0:T(8,128)S(1)}) fusion(f32[384,1152]{1,0:T(8,128)} %fusion.84, f32[384,1152]{1,0:T(8,128)} %fusion.83, f32[384,384]{1,0:T(8,128)S(1)} %copy-done.50, ...), kind=kCustom, calls=%all-reduce-scatter.6 | all-reduce-scatter fusion | flops 3145729 | bytes 9830400
  818.4 39.4 %all-reduce.44 = (f32[768]{0:T(1024)S(1)}, f32[768]{0:T(1024)S(1)}, f32[384]{0:T(512)S(1)}, f32[384]{0:T(512)S(1)}, f32[1536]{0:T(1024)S(1)}, /*index=5*/f32[153...) all-reduce(f32[768]{0:T(1024)S(1)} %pad_maximum_fusion.17, ...), channel_id=29, replica_groups=mesh['dev'=32] {'dev'}, use_global_device_ids=true, to_apply=%region_35.36.clone | all-reduce | flops 9216 | bytes 73728
  963.0 4.9 collective-permute-start.46
  (770 shorter events, 410.7 us)
Async XLA Ops:
  7.2 248.1 %all-gather.29.cloned.1.call-start = ((), (), s32[]{:S(2)}) async-start(), calls=%async_computation.4 | async-start | bytes 2433024 | tf_op jit(solution)/shard_map/all_gather | solution.py:68
  9.0 277.7 %all-gather.31.cloned.1.call-start = ((), (), s32[]{:S(2)}) async-start(), calls=%async_computation.5 | async-start | bytes 1216512 | tf_op jit(solution)/shard_map/all_gather | solution.py:70
  10.5 379.0 %all-gather.33.cloned.1.call-start = ((), (), s32[]{:S(2)}) async-start(), calls=%async_computation.6 | async-start | bytes 2433024 | tf_op jit(solution)/shard_map/all_gather | solution.py:68
  109.1 99.7 %collective-permute-start = (bf16[256,768]{1,0:T(8,128)(2,1)}, bf16[256,768]{1,0:T(8,128)(2,1)}, u32[]{:S(2)}, u32[]{:S(2)}) collective-permute-start(bf16[256,768]{1,0:T(8,128)(2,1)} %get-tuple-element.774), channel_id=1, source_target_pairs={{0,1},{1,2},{2,3},{3,4},{4,5},{5,6},{6,7},{7,8},{8,9},{9,10},{10,1... | collective-permute-start | bytes 1179656 | tf_op jit(solution)/shard_map/ppermute | solution.py:27
  111.3 97.5 %collective-permute-start.1 = (bf16[256,768]{1,0:T(8,128)(2,1)}, bf16[256,768]{1,0:T(8,128)(2,1)}, u32[]{:S(2)}, u32[]{:S(2)}) collective-permute-start(bf16[256,768]{1,0:T(8,128)(2,1)} %get-tuple-element.775), channel_id=1, source_target_pairs={{1,0},{2,1},{3,2},{4,3},{5,4},{6,5},{7,6},{8,7},{9,8},{10,9},{11,1... | collective-permute-start | bytes 1179656 | tf_op jit(solution)/shard_map/ppermute | solution.py:30
  115.5 294.0 %all-gather.35.cloned.1.call-start = ((), (), s32[]{:S(2)}) async-start(), calls=%async_computation.7 | async-start | bytes 1216512 | tf_op jit(solution)/shard_map/all_gather | solution.py:70
  294.5 51.0 %collective-permute-start.2 = (bf16[256,768]{1,0:T(8,128)(2,1)}, bf16[256,768]{1,0:T(8,128)(2,1)}, u32[]{:S(2)}, u32[]{:S(2)}) collective-permute-start(bf16[256,768]{1,0:T(8,128)(2,1)} %get-tuple-element.772), channel_id=1, source_target_pairs={{0,1},{1,2},{2,3},{3,4},{4,5},{5,6},{6,7},{7,8},{8,9},{9,10},{10,1... | collective-permute-start | bytes 1179656 | tf_op jit(solution)/shard_map/ppermute | solution.py:27
  296.8 48.8 %collective-permute-start.3 = (bf16[256,768]{1,0:T(8,128)(2,1)}, bf16[256,768]{1,0:T(8,128)(2,1)}, u32[]{:S(2)}, u32[]{:S(2)}) collective-permute-start(bf16[256,768]{1,0:T(8,128)(2,1)} %get-tuple-element.773), channel_id=1, source_target_pairs={{1,0},{2,1},{3,2},{4,3},{5,4},{6,5},{7,6},{8,7},{9,8},{10,9},{11,1... | collective-permute-start | bytes 1179656 | tf_op jit(solution)/shard_map/ppermute | solution.py:30
  302.4 685.9 %reduce-scatter.17.cloned.1.call-start = ((), (), s32[]{:S(2)}) async-start(), calls=%async_computation.3 | async-start | bytes 2433024 | tf_op jit(solution)/shard_map/reduce_scatter | solution.py:104
  506.1 19.3 %collective-permute-start.4 = (bf16[256,768]{0,1:T(8,128)(2,1)}, bf16[256,768]{0,1:T(8,128)(2,1)}, u32[]{:S(2)}, u32[]{:S(2)}) collective-permute-start(bf16[256,768]{0,1:T(8,128)(2,1)} %get-tuple-element.771), channel_id=1, source_target_pairs={{1,0},{2,1},{3,2},{4,3},{5,4},{6,5},{7,6},{8,7},{9,8},{10,9},{11,1... | collective-permute-start | bytes 1179656 | tf_op jit(solution)/shard_map/ppermute | solution.py:19
  525.3 463.0 %reduce-scatter.15.cloned.1.call-start = ((), (), s32[]{:S(2)}) async-start(), calls=%async_computation.2 | async-start | bytes 2433024 | tf_op jit(solution)/shard_map/reduce_scatter | solution.py:104
  624.2 20.1 %collective-permute-start.6 = (bf16[256,768]{0,1:T(8,128)(2,1)}, bf16[256,768]{0,1:T(8,128)(2,1)}, u32[]{:S(2)}, u32[]{:S(2)}) collective-permute-start(bf16[256,768]{0,1:T(8,128)(2,1)} %get-tuple-element.769), channel_id=1, source_target_pairs={{1,0},{2,1},{3,2},{4,3},{5,4},{6,5},{7,6},{8,7},{9,8},{10,9},{11,1... | collective-permute-start | bytes 1179656 | tf_op jit(solution)/shard_map/ppermute | solution.py:19
  805.8 65.4 %collective-permute-start.38 = (f32[16,384]{1,0:T(8,128)S(1)}, f32[16,384]{1,0:T(8,128)S(1)}, u32[]{:S(2)}, u32[]{:S(2)}) collective-permute-start(f32[16,384]{1,0:T(8,128)S(1)} %get-tuple-element.730), channel_id=1, source_target_pairs={{0,7},{1,8},{2,9},{3,10},{4,11},{5,12},{6,13},{7,14},{8,15},{9,16}... | collective-permute-start | bytes 73736
  807.1 67.5 %collective-permute-start.37 = (f32[16,384]{1,0:T(8,128)S(1)}, f32[16,384]{1,0:T(8,128)S(1)}, u32[]{:S(2)}, u32[]{:S(2)}) collective-permute-start(f32[16,384]{1,0:T(8,128)S(1)} %get-tuple-element.730), channel_id=1, source_target_pairs={{0,6},{1,7},{2,8},{3,9},{4,10},{5,11},{6,12},{7,13},{8,14},{9,15},... | collective-permute-start | bytes 73736
  808.4 69.6 %collective-permute-start.36 = (f32[16,384]{1,0:T(8,128)S(1)}, f32[16,384]{1,0:T(8,128)S(1)}, u32[]{:S(2)}, u32[]{:S(2)}) collective-permute-start(f32[16,384]{1,0:T(8,128)S(1)} %get-tuple-element.730), channel_id=1, source_target_pairs={{0,5},{1,6},{2,7},{3,8},{4,9},{5,10},{6,11},{7,12},{8,13},{9,14},{... | collective-permute-start | bytes 73736
  809.8 55.7 %collective-permute-start.31 = (f32[12,384]{1,0:T(8,128)S(1)}, f32[12,384]{1,0:T(8,128)S(1)}, u32[]{:S(2)}, u32[]{:S(2)}) collective-permute-start(f32[12,384]{1,0:T(8,128)S(1)} %slice.358), channel_id=1, source_target_pairs={{0,8},{1,9},{2,10},{3,11},{4,12},{5,13},{6,14},{7,15},{8,16},{9,17... | collective-permute-start | bytes 55304
  813.1 55.0 %collective-permute-start.39 = (f32[12,384]{1,0:T(8,128)S(1)}, f32[12,384]{1,0:T(8,128)S(1)}, u32[]{:S(2)}, u32[]{:S(2)}) collective-permute-start(f32[12,384]{1,0:T(8,128)S(1)} %slice.359), channel_id=1, source_target_pairs={{0,8},{1,9},{2,10},{3,11},{4,12},{5,13},{6,14},{7,15},{8,16},{9,17... | collective-permute-start | bytes 55304
  865.5 15.8 %collective-permute-start.35 = (f32[16,384]{1,0:T(8,128)S(1)}, f32[16,384]{1,0:T(8,128)S(1)}, u32[]{:S(2)}, u32[]{:S(2)}) collective-permute-start(f32[16,384]{1,0:T(8,128)S(1)} %get-tuple-element.730), channel_id=1, source_target_pairs={{0,4},{1,5},{2,6},{3,7},{4,8},{5,9},{6,10},{7,11},{8,12},{9,13},{1... | collective-permute-start | bytes 73736
  868.1 15.2 %collective-permute-start.34 = (f32[16,384]{1,0:T(8,128)S(1)}, f32[16,384]{1,0:T(8,128)S(1)}, u32[]{:S(2)}, u32[]{:S(2)}) collective-permute-start(f32[16,384]{1,0:T(8,128)S(1)} %get-tuple-element.730), channel_id=1, source_target_pairs={{0,3},{1,4},{2,5},{3,6},{4,7},{5,8},{6,9},{7,10},{8,11},{9,12},{10... | collective-permute-start | bytes 73736
  871.2 15.2 %collective-permute-start.33 = (f32[16,384]{1,0:T(8,128)S(1)}, f32[16,384]{1,0:T(8,128)S(1)}, u32[]{:S(2)}, u32[]{:S(2)}) collective-permute-start(f32[16,384]{1,0:T(8,128)S(1)} %get-tuple-element.730), channel_id=1, source_target_pairs={{0,2},{1,3},{2,4},{3,5},{4,6},{5,7},{6,8},{7,9},{8,10},{9,11},{10,... | collective-permute-start | bytes 73736
  874.7 14.6 %collective-permute-start.32 = (f32[16,384]{1,0:T(8,128)S(1)}, f32[16,384]{1,0:T(8,128)S(1)}, u32[]{:S(2)}, u32[]{:S(2)}) collective-permute-start(f32[16,384]{1,0:T(8,128)S(1)} %get-tuple-element.730), channel_id=1, source_target_pairs={{0,1},{1,2},{2,3},{3,4},{4,5},{5,6},{6,7},{7,8},{8,9},{9,10},{10,1... | collective-permute-start | bytes 73736
  889.3 15.4 %collective-permute-start.26 = (f32[16,384]{1,0:T(8,128)S(1)}, f32[16,384]{1,0:T(8,128)S(1)}, u32[]{:S(2)}, u32[]{:S(2)}) collective-permute-start(f32[16,384]{1,0:T(8,128)S(1)} %get-tuple-element.731), channel_id=1, source_target_pairs={{0,3},{1,4},{2,5},{3,6},{4,7},{5,8},{6,9},{7,10},{8,11},{9,12},{10... | collective-permute-start | bytes 73736
  892.1 16.6 %collective-permute-start.25 = (f32[16,384]{1,0:T(8,128)S(1)}, f32[16,384]{1,0:T(8,128)S(1)}, u32[]{:S(2)}, u32[]{:S(2)}) collective-permute-start(f32[16,384]{1,0:T(8,128)S(1)} %get-tuple-element.731), channel_id=1, source_target_pairs={{0,2},{1,3},{2,4},{3,5},{4,6},{5,7},{6,8},{7,9},{8,10},{9,11},{10,... | collective-permute-start | bytes 73736
  894.6 15.4 %collective-permute-start.24 = (f32[16,384]{1,0:T(8,128)S(1)}, f32[16,384]{1,0:T(8,128)S(1)}, u32[]{:S(2)}, u32[]{:S(2)}) collective-permute-start(f32[16,384]{1,0:T(8,128)S(1)} %get-tuple-element.731), channel_id=1, source_target_pairs={{0,1},{1,2},{2,3},{3,4},{4,5},{5,6},{6,7},{7,8},{8,9},{9,10},{10,1... | collective-permute-start | bytes 73736
  896.6 16.4 %collective-permute-start.15 = (f32[12,1152]{1,0:T(8,128)S(1)}, f32[12,1152]{1,0:T(8,128)S(1)}, u32[]{:S(2)}, u32[]{:S(2)}) collective-permute-start(f32[12,1152]{1,0:T(8,128)S(1)} %slice.356), channel_id=1, source_target_pairs={{0,8},{1,9},{2,10},{3,11},{4,12},{5,13},{6,14},{7,15},{8,16},{9,17... | collective-permute-start | bytes 165896
  898.2 17.0 %collective-permute-start.23 = (f32[12,1152]{1,0:T(8,128)S(1)}, f32[12,1152]{1,0:T(8,128)S(1)}, u32[]{:S(2)}, u32[]{:S(2)}) collective-permute-start(f32[12,1152]{1,0:T(8,128)S(1)} %slice.357), channel_id=1, source_target_pairs={{0,8},{1,9},{2,10},{3,11},{4,12},{5,13},{6,14},{7,15},{8,16},{9,17... | collective-permute-start | bytes 165896
  940.6 16.8 %collective-permute-start.54 = (f32[16,1536]{1,0:T(8,128)S(1)}, f32[16,1536]{1,0:T(8,128)S(1)}, u32[]{:S(2)}, u32[]{:S(2)}) collective-permute-start(f32[16,1536]{1,0:T(8,128)S(1)} %get-tuple-element.732), channel_id=1, source_target_pairs={{0,7},{1,8},{2,9},{3,10},{4,11},{5,12},{6,13},{7,14},{8,15},{9,16}... | collective-permute-start | bytes 294920
  942.8 17.6 %collective-permute-start.53 = (f32[16,1536]{1,0:T(8,128)S(1)}, f32[16,1536]{1,0:T(8,128)S(1)}, u32[]{:S(2)}, u32[]{:S(2)}) collective-permute-start(f32[16,1536]{1,0:T(8,128)S(1)} %get-tuple-element.732), channel_id=1, source_target_pairs={{0,6},{1,7},{2,8},{3,9},{4,10},{5,11},{6,12},{7,13},{8,14},{9,15},... | collective-permute-start | bytes 294920
  945.0 18.0 %collective-permute-start.52 = (f32[16,1536]{1,0:T(8,128)S(1)}, f32[16,1536]{1,0:T(8,128)S(1)}, u32[]{:S(2)}, u32[]{:S(2)}) collective-permute-start(f32[16,1536]{1,0:T(8,128)S(1)} %get-tuple-element.732), channel_id=1, source_target_pairs={{0,5},{1,6},{2,7},{3,8},{4,9},{5,10},{6,11},{7,12},{8,13},{9,14},{... | collective-permute-start | bytes 294920
  947.1 20.9 %collective-permute-start.51 = (f32[16,1536]{1,0:T(8,128)S(1)}, f32[16,1536]{1,0:T(8,128)S(1)}, u32[]{:S(2)}, u32[]{:S(2)}) collective-permute-start(f32[16,1536]{1,0:T(8,128)S(1)} %get-tuple-element.732), channel_id=1, source_target_pairs={{0,4},{1,5},{2,6},{3,7},{4,8},{5,9},{6,10},{7,11},{8,12},{9,13},{1... | collective-permute-start | bytes 294920
  954.3 15.6 %collective-permute-start.50 = (f32[16,1536]{1,0:T(8,128)S(1)}, f32[16,1536]{1,0:T(8,128)S(1)}, u32[]{:S(2)}, u32[]{:S(2)}) collective-permute-start(f32[16,1536]{1,0:T(8,128)S(1)} %get-tuple-element.732), channel_id=1, source_target_pairs={{0,3},{1,4},{2,5},{3,6},{4,7},{5,8},{6,9},{7,10},{8,11},{9,12},{10... | collective-permute-start | bytes 294920
  957.4 14.7 %collective-permute-start.49 = (f32[16,1536]{1,0:T(8,128)S(1)}, f32[16,1536]{1,0:T(8,128)S(1)}, u32[]{:S(2)}, u32[]{:S(2)}) collective-permute-start(f32[16,1536]{1,0:T(8,128)S(1)} %get-tuple-element.732), channel_id=1, source_target_pairs={{0,2},{1,3},{2,4},{3,5},{4,6},{5,7},{6,8},{7,9},{8,10},{9,11},{10,... | collective-permute-start | bytes 294920
  (197 other events, 1806.5 us)
Sparse Core Ops, SparseCore 0:
  11.5 58.8 all-gather.28
  73.8 54.1 all-gather.30
  131.5 57.4 all-gather.32
  302.5 51.7 all-gather.34
  525.4 97.9 reduce-scatter.16
  644.4 105.6 reduce-scatter.14
where the time goes:
time: 1010 us; the launch traced here: 997 us
  blocking collectives  394 us (39%)
  matrix products  213 us (21%)
  starting transfers between devices  141 us (14%)
  local copies, waits for them, and re-layouts  112 us (11%)
  other arithmetic  105 us (10%)
  between operations  17.4 us (2%)
  waiting for transfers between devices  10.7 us (1%)
    unnamed x3, blocking collectives  227 us
    unnamed x48, starting transfers between devices  112 us
    all_gather x2, blocking collectives, fetch_forward(): lax.all_gather(shards[0], 'dev', axis=0, tiled=True)  87.5 us
    all_gather x2, blocking collectives, fetch_forward(): lax.all_gather(shards[2], 'dev', axis=0, tiled=True)  80.1 us
    dot_general x8, matrix products, product(): return jnp.dot(left, right, preferred_element_type=jnp.float32)  66.5 us
    dot_general x8, matrix products, contract_last(): lax.dot_general(left, right, (((1,), (1,)), ((), ())), preferred_element_...  33.1 us
    unnamed x303, local copies, waits for them, and re-layouts  31.2 us
    dot_general x4, matrix products, one_block(): jnp.einsum('qhd,khd->hqk', grad_block, value_heads, preferred_element_typ...  28.6 us
  transfers between devices with their start and end apart: 62, of which 5 were waited for; matrix products, arithmetic and copies ran while one was open for 47% of the time, Pallas kernels for 0%

commit v1 on v0

--- a/solution.py
+++ b/solution.py
@@ -61,7 +61,15 @@
 
 def fetch_forward(shards):
     return (
-        lax.all_gather(shards[0], "dev", axis=0, tiled=True),
+        jnp.concatenate(
+            lax.all_to_all(
+                jnp.stack(lax.axis_size("dev") * [shards[0]], axis=0),
+                axis_name="dev",
+                split_axis=0,
+                concat_axis=0,
+            ),
+            0,
+        ),
         lax.all_gather(shards[1], "dev", axis=0, tiled=True),
         lax.all_gather(shards[2], "dev", axis=0, tiled=True),
         lax.all_gather(shards[3], "dev", axis=0, tiled=True),

time: 1010 us -> 1110 us (1.099)
  matrix products: 213 us -> 245 us
  starting transfers between devices: 141 us -> 165 us
  other arithmetic: 105 us -> 124 us
  blocking collectives: 394 us -> 412 us
    dot_general x8, matrix products: 17 us -> 35.3 us  [block_scores(): jnp.einsum('qhd,khd->hqk', query_block, key_heads, preferred_element_type...]
    dot_general x4, matrix products: 28.6 us -> 45.3 us  [one_block(): jnp.einsum('qhd,khd->hqk', grad_block, value_heads, preferred_element_typ...]
    all_to_all x0 -> x2, starting transfers between devices: none -> 13 us  [fetch_forward(): lax.all_to_all(jnp.stack(lax.axis_size('dev') * [shards[0]], axis=0), axi...]
    all_gather x2, blocking collectives: 87.5 us -> 98.9 us  [fetch_backward(): lax.all_gather(shards[0], 'dev', axis=0, tiled=True)]
    unnamed x303 -> x341, local copies, waits for them, and re-layouts: 31.2 us -> 28.2 us
  transfers between devices with their start and end apart: 62 -> 64, of which waited for: 5 -> 4; matrix products, arithmetic and copies ran while one was open for 47% -> 45% of each run, Pallas kernels for 0% -> 0%
where the time goes in v1:
time: 1110 us; the launch traced here: 1090 us
  blocking collectives  412 us (37%)
  matrix products  245 us (22%)
  starting transfers between devices  165 us (15%)
  other arithmetic  124 us (11%)
  local copies, waits for them, and re-layouts  113 us (10%)
  between operations  17.4 us (2%)
  waiting for transfers between devices  11.4 us (1%)
    unnamed x3, blocking collectives  231 us
    unnamed x48, starting transfers between devices  123 us
    all_gather x2, blocking collectives, fetch_backward(): lax.all_gather(shards[0], 'dev', axis=0, tiled=True)  98.9 us
    all_gather x2, blocking collectives, fetch_forward(): lax.all_gather(shards[2], 'dev', axis=0, tiled=True)  81.6 us
    dot_general x8, matrix products, product(): return jnp.dot(left, right, preferred_element_type=jnp.float32)  57 us
    dot_general x4, matrix products, one_block(): jnp.einsum('qhd,khd->hqk', grad_block, value_heads, preferred_element_typ...  45.3 us
    dot_general x8, matrix products, contract_last(): lax.dot_general(left, right, (((1,), (1,)), ((), ())), preferred_element_...  35.7 us
    dot_general x8, matrix products, block_scores(): jnp.einsum('qhd,khd->hqk', query_block, key_heads, preferred_element_type...  35.3 us
  transfers between devices with their start and end apart: 64, of which 4 were waited for; matrix products, arithmetic and copies ran while one was open for 45% of the time, Pallas kernels for 0%

profile of v1, /device:TPU:4, one launch (start us, length us, event | category | flops | bytes accessed | tf_op | source)
XLA Modules:
  0.0 1092.2 jit_solution(12618393640605026851)
XLA Ops:
  14.8 6.1 all-to-all-start
  25.3 50.8 %all-reduce.45 = (bf16[768]{0:T(1024)(128)(2,1)}, bf16[768]{0:T(1024)(128)(2,1)}, bf16[384]{0:T(512)(128)(2,1)S(1)}, bf16[384]{0:T(512)(128)(2,1)S(1)}, bf16[384...) all-reduce(bf16[768]{0:T(1024)(128)(2,1)S(1)} %dynamic-update-slice, ...), channel_id=4, replica_groups=mesh['dev'=32] {'dev'}, use_global_device_ids=true, to_apply=%add.2 | all-reduce | flops 9216 | bytes 36864
  95.6 40.5 %all-gather.3 = bf16[1,384,384]{2,0,1:T(2,128)(2,1)} all-gather(bf16[1,12,384]{2,0,1:T(2,128)(2,1)S(1)} %get-tuple-element.784), channel_id=5, replica_groups=mesh['dev'=32] {'dev'}, dimensions={1}, use_global_device_ids=true | all-gather | bytes 304128 | tf_op jit(solution)/shard_map/all_gather | solution.py:74
  136.1 41.1 %all-gather.14 = bf16[1,384,384]{2,0,1:T(2,128)(2,1)} all-gather(bf16[1,12,384]{2,0,1:T(2,128)(2,1)S(1)} %get-tuple-element.783), channel_id=16, replica_groups=mesh['dev'=32] {'dev'}, dimensions={1}, use_global_device_ids=true | all-gather | bytes 304128 | tf_op jit(solution)/shard_map/all_gather | solution.py:74
  178.4 6.9 all-to-all-start.1
  198.5 54.7 %all-gather.22 = bf16[1,384,1152]{2,0,1:T(2,128)(2,1)} all-gather(bf16[1,12,1152]{2,0,1:T(2,128)(2,1)S(1)} %copy-done.59), channel_id=24, replica_groups=mesh['dev'=32] {'dev'}, dimensions={1}, use_global_device_ids=true | all-gather | bytes 912384 | tf_op jit(solution)/shard_map/all_gather | solution.py:89
  263.2 28.8 %while.58 = (s32[]{:T(128)}, bf16[2,512,384]{2,1,0:T(8,128)(2,1)}, f32[2,6,512]{2,1,0:T(8,128)S(1)}, s32[2]{0:T(128)S(1)}, bf16[1536,768]{0,1:T(8,128)(2,1)S(1)}...) while((s32[]{:T(128)}, bf16[2,512,384]{2,1,0:T(8,128)(2,1)}, ...), condition=%wide.region_5.6_spmd, body=%wide.region_2.5_spmd.sunk | while | flops 843772928 | bytes 50985752 | solution.py:159
  296.5 19.5 %multiply_convert_fusion.3 = (bf16[1024,1536]{1,0:T(8,128)(2,1)}, f32[1024,1536]{1,0:T(8,128)}, f32[1024,1536]{1,0:T(8,128)}) fusion(f32[1536]{0:T(1024)S(1)} %copy-done.119, bf16[1,384,1536]{2,0,1:T(2,128)(2,1)} %all-gather.29.cloned.1.call-done, f32[1024,384]{0,1:T(8,128)} %copy-done.18, f32[384]{0:T(512)S(1)} %copy-done.128, f32[384]{0:T(512)S(1)} %copy-done.102, ...), kind=kOutput, calls=%fused_computation.85 | convolution fusion | flops 1313734656 | bytes 18498560 | tf_op jit(solution)/shard_map/dot_general | solution.py:43
  330.8 44.2 %all-gather.23 = bf16[1,384,1152]{2,0,1:T(2,128)(2,1)} all-gather(bf16[1,12,1152]{2,0,1:T(2,128)(2,1)S(1)} %copy-done.58), channel_id=25, replica_groups=mesh['dev'=32] {'dev'}, dimensions={1}, use_global_device_ids=true | all-gather | bytes 912384 | tf_op jit(solution)/shard_map/all_gather | solution.py:89
  383.0 28.7 %while.59 = (s32[]{:T(128)}, bf16[2,512,384]{2,1,0:T(8,128)(2,1)}, f32[2,6,512]{2,1,0:T(8,128)S(1)}, s32[2]{0:T(128)S(1)}, bf16[1536,768]{0,1:T(8,128)(2,1)S(1)}...) while((s32[]{:T(128)}, bf16[2,512,384]{2,1,0:T(8,128)(2,1)}, ...), condition=%wide.region_13.14_spmd, body=%wide.region_10.13_spmd.sunk | while | flops 843772928 | bytes 50985752 | solution.py:159
  415.8 19.6 %multiply_convert_fusion.2 = (bf16[1024,1536]{1,0:T(8,128)(2,1)}, f32[1024,1536]{1,0:T(8,128)}, f32[1024,1536]{1,0:T(8,128)}) fusion(f32[1536]{0:T(1024)S(1)} %copy-done.121, bf16[1,384,1536]{2,0,1:T(2,128)(2,1)} %all-gather.33.cloned.1.call-done, f32[1024,384]{0,1:T(8,128)} %copy-done.21, f32[384]{0:T(512)S(1)} %copy-done.131, f32[384]{0:T(512)S(1)} %copy-done.107, ...), kind=kOutput, calls=%fused_computation.72 | convolution fusion | flops 1313734656 | bytes 18498560 | tf_op jit(solution)/shard_map/dot_general | solution.py:43
  435.4 7.8 convert_reduce_fusion
  460.3 85.7 %while.60 = (s32[]{:T(128)}, bf16[1024,384]{0,1:T(8,128)(2,1)}, f32[1536,768]{0,1:T(8,128)}, bf16[1536,768]{0,1:T(8,128)(2,1)S(1)}, s32[1024]{0:T(1024)S(1)}, /*...) while((s32[]{:T(128)}, bf16[1024,384]{0,1:T(8,128)(2,1)}, ...), condition=%wide.region_20.21_spmd, body=%wide.region_18.20_spmd.sunk | while | flops 2063332352 | bytes 199465520 | solution.py:211
  462.5 6.4 fusion.253
  473.8 11.3 %multiply_reduce_fusion.13 = (f32[6,512]{1,0:T(8,128)S(1)}, f32[6,512,1024]{2,1,0:T(8,128)}) fusion(f32[6,512,1024]{2,1,0:T(8,128)} %fusion.253, f32[6,512]{1,0:T(8,128)S(1)} %dynamic-slice_bitcast_fusion.26, pred[512,1024]{1,0:T(8,128)(4,1)} %broadcast_compare_fusion.10, bf16[512,6,64]{0,2,1:T(8,128)(2,1)} %bitcast.370, ...), kind=kOutput, calls=%fused_computation.29.clone.1 | convolution fusion | flops 418378752 | bytes 26894336 | tf_op jit(solution)/shard_map/while/body/eval_jaxpr/qhd,khd->hqk/dot_general | solution.py:177
  485.2 6.9 multiply_convert_fusion.6
  505.2 6.4 fusion.253
  516.5 11.3 %multiply_reduce_fusion.13 = (f32[6,512]{1,0:T(8,128)S(1)}, f32[6,512,1024]{2,1,0:T(8,128)}) fusion(f32[6,512,1024]{2,1,0:T(8,128)} %fusion.253, f32[6,512]{1,0:T(8,128)S(1)} %dynamic-slice_bitcast_fusion.26, pred[512,1024]{1,0:T(8,128)(4,1)} %broadcast_compare_fusion.10, bf16[512,6,64]{0,2,1:T(8,128)(2,1)} %bitcast.370, ...), kind=kOutput, calls=%fused_computation.29.clone.1 | convolution fusion | flops 418378752 | bytes 26894336 | tf_op jit(solution)/shard_map/while/body/eval_jaxpr/qhd,khd->hqk/dot_general | solution.py:177
  527.8 6.9 multiply_convert_fusion.6
  557.8 6.6 collective-permute-start.4
  581.3 5.0 fusion.137
  591.6 8.1 convert_reduce_fusion.1
  614.2 86.0 %while.61 = (s32[]{:T(128)}, bf16[1024,384]{0,1:T(8,128)(2,1)}, f32[1536,768]{0,1:T(8,128)}, bf16[1536,768]{0,1:T(8,128)(2,1)S(1)}, s32[1024]{0:T(1024)S(1)}, /*...) while((s32[]{:T(128)}, bf16[1024,384]{0,1:T(8,128)(2,1)}, ...), condition=%wide.region_27.28_spmd, body=%wide.region_25.27_spmd.sunk | while | flops 2063332352 | bytes 199465520 | solution.py:211
  616.5 6.4 fusion.267
  627.9 11.4 %multiply_reduce_fusion.14 = (f32[6,512]{1,0:T(8,128)S(1)}, f32[6,512,1024]{2,1,0:T(8,128)}) fusion(f32[6,512,1024]{2,1,0:T(8,128)} %fusion.267, f32[6,512]{1,0:T(8,128)S(1)} %dynamic-slice_bitcast_fusion.27, pred[512,1024]{1,0:T(8,128)(4,1)} %broadcast_compare_fusion.11, bf16[512,6,64]{0,2,1:T(8,128)(2,1)} %bitcast.372, ...), kind=kOutput, calls=%fused_computation.47.clone.1 | convolution fusion | flops 418378752 | bytes 26894336 | tf_op jit(solution)/shard_map/while/body/eval_jaxpr/qhd,khd->hqk/dot_general | solution.py:177
  639.4 6.9 multiply_convert_fusion.7
  659.4 6.4 fusion.267
  670.8 11.3 %multiply_reduce_fusion.14 = (f32[6,512]{1,0:T(8,128)S(1)}, f32[6,512,1024]{2,1,0:T(8,128)}) fusion(f32[6,512,1024]{2,1,0:T(8,128)} %fusion.267, f32[6,512]{1,0:T(8,128)S(1)} %dynamic-slice_bitcast_fusion.27, pred[512,1024]{1,0:T(8,128)(4,1)} %broadcast_compare_fusion.11, bf16[512,6,64]{0,2,1:T(8,128)(2,1)} %bitcast.372, ...), kind=kOutput, calls=%fused_computation.47.clone.1 | convolution fusion | flops 418378752 | bytes 26894336 | tf_op jit(solution)/shard_map/while/body/eval_jaxpr/qhd,khd->hqk/dot_general | solution.py:177
  682.1 6.9 multiply_convert_fusion.7
  742.5 140.9 %fusion.117 = (f32[16,1152]{1,0:T(8,128)}, f32[16,1152]{1,0:T(8,128)}, f32[16,384]{1,0:T(8,128)}, f32[16,384]{1,0:T(8,128)}, f32[16,1536]{1,0:T(8,128)}, /*index=5*/f32[16,1536]{1,0:T(8,128)}) fusion(f32[384,1152]{1,0:T(8,128)} %fusion.82, f32[384,1152]{1,0:T(8,128)} %fusion.81, f32[384,384]{1,0:T(8,128)S(1)} %copy-done.47, f32[384,384]{1,0:T(8,128)S(1)} %fusion.143, ...), kind=kCustom, calls=%all-reduce-scatter.6 | all-reduce-scatter fusion | flops 3145729 | bytes 9830400
  891.0 5.9 collective-permute-start.26
  911.2 39.5 %all-reduce.44 = (f32[768]{0:T(1024)S(1)}, f32[768]{0:T(1024)S(1)}, f32[384]{0:T(512)S(1)}, f32[384]{0:T(512)S(1)}, f32[1536]{0:T(1024)S(1)}, /*index=5*/f32[153...) all-reduce(f32[768]{0:T(1024)S(1)} %pad_maximum_fusion.17, ...), channel_id=29, replica_groups=mesh['dev'=32] {'dev'}, use_global_device_ids=true, to_apply=%region_35.36.clone | all-reduce | flops 9216 | bytes 73728
  (820 shorter events, 474.9 us)
Async XLA Ops:
  7.3 289.2 %all-gather.29.cloned.1.call-start = ((), (), s32[]{:S(2)}) async-start(), calls=%async_computation.6 | async-start | bytes 2433024 | tf_op jit(solution)/shard_map/all_gather | solution.py:76
  9.1 307.0 %all-gather.31.cloned.1.call-start = ((), (), s32[]{:S(2)}) async-start(), calls=%async_computation.7 | async-start | bytes 1216512 | tf_op jit(solution)/shard_map/all_gather | solution.py:78
  10.7 405.0 %all-gather.33.cloned.1.call-start = ((), (), s32[]{:S(2)}) async-start(), calls=%async_computation.8 | async-start | bytes 2433024 | tf_op jit(solution)/shard_map/all_gather | solution.py:76
  14.8 162.6 %all-to-all-start = ((bf16[32,12,1152]{2,1,0:T(8,128)(2,1)}), bf16[32,12,1152]{2,1,0:T(8,128)(2,1)S(1)}, u32[]{:S(2)}, u32[]{:S(2)}) async-start(bf16[32,12,1152]{2,1,0:T(8,128)(2,1)} %stack.114), calls=%async_computation | async-start | bytes 2359296 | tf_op jit(solution)/shard_map/all_to_all | solution.py:65
  20.9 414.5 %all-gather.35.cloned.1.call-start = ((), (), s32[]{:S(2)}) async-start(), calls=%async_computation.9 | async-start | bytes 1216512 | tf_op jit(solution)/shard_map/all_gather | solution.py:78
  178.4 77.1 %all-to-all-start.1 = ((bf16[32,12,1152]{2,1,0:T(8,128)(2,1)}), bf16[32,12,1152]{2,1,0:T(8,128)(2,1)S(1)}, u32[]{:S(2)}, u32[]{:S(2)}) async-start(bf16[32,12,1152]{2,1,0:T(8,128)(2,1)} %stack.115), calls=%async_computation.1 | async-start | bytes 2359296 | tf_op jit(solution)/shard_map/all_to_all | solution.py:65
  185.4 897.9 %reduce-scatter.17.cloned.1.call-start = ((), (), s32[]{:S(2)}) async-start(), calls=%async_computation.5 | async-start | bytes 2433024 | tf_op jit(solution)/shard_map/reduce_scatter | solution.py:112
  192.0 64.6 %collective-permute-start = (bf16[256,768]{1,0:T(8,128)(2,1)}, bf16[256,768]{1,0:T(8,128)(2,1)S(1)}, u32[]{:S(2)}, u32[]{:S(2)}) collective-permute-start(bf16[256,768]{1,0:T(8,128)(2,1)} %get-tuple-element.774), channel_id=1, source_target_pairs={{0,1},{1,2},{2,3},{3,4},{4,5},{5,6},{6,7},{7,8},{8,9},{9,10},{10,1... | collective-permute-start | bytes 1179656 | tf_op jit(solution)/shard_map/ppermute | solution.py:27
  194.0 62.6 %collective-permute-start.1 = (bf16[256,768]{1,0:T(8,128)(2,1)}, bf16[256,768]{1,0:T(8,128)(2,1)}, u32[]{:S(2)}, u32[]{:S(2)}) collective-permute-start(bf16[256,768]{1,0:T(8,128)(2,1)} %get-tuple-element.775), channel_id=1, source_target_pairs={{1,0},{2,1},{3,2},{4,3},{5,4},{6,5},{7,6},{8,7},{9,8},{10,9},{11,1... | collective-permute-start | bytes 1179656 | tf_op jit(solution)/shard_map/ppermute | solution.py:30
  324.4 51.8 %collective-permute-start.2 = (bf16[256,768]{1,0:T(8,128)(2,1)}, bf16[256,768]{1,0:T(8,128)(2,1)S(1)}, u32[]{:S(2)}, u32[]{:S(2)}) collective-permute-start(bf16[256,768]{1,0:T(8,128)(2,1)} %get-tuple-element.772), channel_id=1, source_target_pairs={{0,1},{1,2},{2,3},{3,4},{4,5},{5,6},{6,7},{7,8},{8,9},{9,10},{10,1... | collective-permute-start | bytes 1179656 | tf_op jit(solution)/shard_map/ppermute | solution.py:27
  326.6 49.6 %collective-permute-start.3 = (bf16[256,768]{1,0:T(8,128)(2,1)S(1)}, bf16[256,768]{1,0:T(8,128)(2,1)}, u32[]{:S(2)}, u32[]{:S(2)}) collective-permute-start(bf16[256,768]{1,0:T(8,128)(2,1)S(1)} %get-tuple-element.773), channel_id=1, source_target_pairs={{1,0},{2,1},{3,2},{4,3},{5,4},{6,5},{7,6},{8,7},{9,8},{10,9},{11,1... | collective-permute-start | bytes 1179656 | tf_op jit(solution)/shard_map/ppermute | solution.py:30
  557.8 16.8 %collective-permute-start.4 = (bf16[256,768]{0,1:T(8,128)(2,1)S(1)}, bf16[256,768]{0,1:T(8,128)(2,1)}, u32[]{:S(2)}, u32[]{:S(2)}) collective-permute-start(bf16[256,768]{0,1:T(8,128)(2,1)S(1)} %get-tuple-element.771), channel_id=1, source_target_pairs={{1,0},{2,1},{3,2},{4,3},{5,4},{6,5},{7,6},{8,7},{9,8},{10,9},{11,1... | collective-permute-start | bytes 1179656 | tf_op jit(solution)/shard_map/ppermute | solution.py:19
  569.7 513.7 %reduce-scatter.15.cloned.1.call-start = ((), (), s32[]{:S(2)}) async-start(), calls=%async_computation.4 | async-start | bytes 2433024 | tf_op jit(solution)/shard_map/reduce_scatter | solution.py:112
  703.0 23.0 %collective-permute-start.6 = (bf16[256,768]{0,1:T(8,128)(2,1)S(1)}, bf16[256,768]{0,1:T(8,128)(2,1)}, u32[]{:S(2)}, u32[]{:S(2)}) collective-permute-start(bf16[256,768]{0,1:T(8,128)(2,1)S(1)} %get-tuple-element.769), channel_id=1, source_target_pairs={{1,0},{2,1},{3,2},{4,3},{5,4},{6,5},{7,6},{8,7},{9,8},{10,9},{11,1... | collective-permute-start | bytes 1179656 | tf_op jit(solution)/shard_map/ppermute | solution.py:19
  884.1 80.4 %collective-permute-start.24 = (f32[16,384]{1,0:T(8,128)}, f32[16,384]{1,0:T(8,128)S(1)}, u32[]{:S(2)}, u32[]{:S(2)}) collective-permute-start(f32[16,384]{1,0:T(8,128)} %get-tuple-element.731), channel_id=1, source_target_pairs={{0,1},{1,2},{2,3},{3,4},{4,5},{5,6},{6,7},{7,8},{8,9},{9,10},{10,1... | collective-permute-start | bytes 73736
  886.8 82.7 %collective-permute-start.25 = (f32[16,384]{1,0:T(8,128)}, f32[16,384]{1,0:T(8,128)S(1)}, u32[]{:S(2)}, u32[]{:S(2)}) collective-permute-start(f32[16,384]{1,0:T(8,128)} %get-tuple-element.731), channel_id=1, source_target_pairs={{0,2},{1,3},{2,4},{3,5},{4,6},{5,7},{6,8},{7,9},{8,10},{9,11},{10,... | collective-permute-start | bytes 73736
  891.0 81.3 %collective-permute-start.26 = (f32[16,384]{1,0:T(8,128)}, f32[16,384]{1,0:T(8,128)S(1)}, u32[]{:S(2)}, u32[]{:S(2)}) collective-permute-start(f32[16,384]{1,0:T(8,128)} %get-tuple-element.731), channel_id=1, source_target_pairs={{0,3},{1,4},{2,5},{3,6},{4,7},{5,8},{6,9},{7,10},{8,11},{9,12},{10... | collective-permute-start | bytes 73736
  905.1 53.5 %collective-permute-start.31 = (f32[12,384]{1,0:T(8,128)S(1)}, f32[12,384]{1,0:T(8,128)S(1)}, u32[]{:S(2)}, u32[]{:S(2)}) collective-permute-start(f32[12,384]{1,0:T(8,128)S(1)} %slice.364), channel_id=1, source_target_pairs={{0,8},{1,9},{2,10},{3,11},{4,12},{5,13},{6,14},{7,15},{8,16},{9,17... | collective-permute-start | bytes 55304
  906.4 55.2 %collective-permute-start.39 = (f32[12,384]{1,0:T(8,128)S(1)}, f32[12,384]{1,0:T(8,128)S(1)}, u32[]{:S(2)}, u32[]{:S(2)}) collective-permute-start(f32[12,384]{1,0:T(8,128)S(1)} %slice.365), channel_id=1, source_target_pairs={{0,8},{1,9},{2,10},{3,11},{4,12},{5,13},{6,14},{7,15},{8,16},{9,17... | collective-permute-start | bytes 55304
  958.5 15.7 %collective-permute-start.27 = (f32[16,384]{1,0:T(8,128)S(1)}, f32[16,384]{1,0:T(8,128)S(1)}, u32[]{:S(2)}, u32[]{:S(2)}) collective-permute-start(f32[16,384]{1,0:T(8,128)S(1)} %copy-done.69), channel_id=1, source_target_pairs={{0,4},{1,5},{2,6},{3,7},{4,8},{5,9},{6,10},{7,11},{8,12},{9,13},{1... | collective-permute-start | bytes 73736
  961.6 15.6 %collective-permute-start.28 = (f32[16,384]{1,0:T(8,128)S(1)}, f32[16,384]{1,0:T(8,128)S(1)}, u32[]{:S(2)}, u32[]{:S(2)}) collective-permute-start(f32[16,384]{1,0:T(8,128)S(1)} %copy-done.69), channel_id=1, source_target_pairs={{0,5},{1,6},{2,7},{3,8},{4,9},{5,10},{6,11},{7,12},{8,13},{9,14},{... | collective-permute-start | bytes 73736
  964.4 16.4 %collective-permute-start.29 = (f32[16,384]{1,0:T(8,128)S(1)}, f32[16,384]{1,0:T(8,128)S(1)}, u32[]{:S(2)}, u32[]{:S(2)}) collective-permute-start(f32[16,384]{1,0:T(8,128)S(1)} %copy-done.69), channel_id=1, source_target_pairs={{0,6},{1,7},{2,8},{3,9},{4,10},{5,11},{6,12},{7,13},{8,14},{9,15},... | collective-permute-start | bytes 73736
  989.8 15.6 %collective-permute-start.15 = (f32[12,1152]{1,0:T(8,128)S(1)}, f32[12,1152]{1,0:T(8,128)S(1)}, u32[]{:S(2)}, u32[]{:S(2)}) collective-permute-start(f32[12,1152]{1,0:T(8,128)S(1)} %slice.362), channel_id=1, source_target_pairs={{0,8},{1,9},{2,10},{3,11},{4,12},{5,13},{6,14},{7,15},{8,16},{9,17... | collective-permute-start | bytes 165896
  991.1 16.5 %collective-permute-start.23 = (f32[12,1152]{1,0:T(8,128)S(1)}, f32[12,1152]{1,0:T(8,128)S(1)}, u32[]{:S(2)}, u32[]{:S(2)}) collective-permute-start(f32[12,1152]{1,0:T(8,128)S(1)} %slice.363), channel_id=1, source_target_pairs={{0,8},{1,9},{2,10},{3,11},{4,12},{5,13},{6,14},{7,15},{8,16},{9,17... | collective-permute-start | bytes 165896
  997.0 19.1 %collective-permute-start.10 = (f32[16,1152]{1,0:T(8,128)S(1)}, f32[16,1152]{1,0:T(8,128)S(1)}, u32[]{:S(2)}, u32[]{:S(2)}) collective-permute-start(f32[16,1152]{1,0:T(8,128)S(1)} %copy-done.56), channel_id=1, source_target_pairs={{0,3},{1,4},{2,5},{3,6},{4,7},{5,8},{6,9},{7,10},{8,11},{9,12},{10... | collective-permute-start | bytes 221192
  998.9 19.1 %collective-permute-start.11 = (f32[16,1152]{1,0:T(8,128)S(1)}, f32[16,1152]{1,0:T(8,128)S(1)}, u32[]{:S(2)}, u32[]{:S(2)}) collective-permute-start(f32[16,1152]{1,0:T(8,128)S(1)} %copy-done.56), channel_id=1, source_target_pairs={{0,4},{1,5},{2,6},{3,7},{4,8},{5,9},{6,10},{7,11},{8,12},{9,13},{1... | collective-permute-start | bytes 221192
  1002.7 18.3 %collective-permute-start.12 = (f32[16,1152]{1,0:T(8,128)S(1)}, f32[16,1152]{1,0:T(8,128)S(1)}, u32[]{:S(2)}, u32[]{:S(2)}) collective-permute-start(f32[16,1152]{1,0:T(8,128)S(1)} %copy-done.56), channel_id=1, source_target_pairs={{0,5},{1,6},{2,7},{3,8},{4,9},{5,10},{6,11},{7,12},{8,13},{9,14},{... | collective-permute-start | bytes 221192
  1005.4 19.2 %collective-permute-start.13 = (f32[16,1152]{1,0:T(8,128)S(1)}, f32[16,1152]{1,0:T(8,128)S(1)}, u32[]{:S(2)}, u32[]{:S(2)}) collective-permute-start(f32[16,1152]{1,0:T(8,128)S(1)} %copy-done.56), channel_id=1, source_target_pairs={{0,6},{1,7},{2,8},{3,9},{4,10},{5,11},{6,12},{7,13},{8,14},{9,15},... | collective-permute-start | bytes 221192
  1039.0 17.6 %collective-permute-start.40 = (f32[16,1536]{1,0:T(8,128)S(1)}, f32[16,1536]{1,0:T(8,128)S(1)}, u32[]{:S(2)}, u32[]{:S(2)}) collective-permute-start(f32[16,1536]{1,0:T(8,128)S(1)} %copy-done.50), channel_id=1, source_target_pairs={{0,1},{1,2},{2,3},{3,4},{4,5},{5,6},{6,7},{7,8},{8,9},{9,10},{10,1... | collective-permute-start | bytes 294920
  1040.9 19.7 %collective-permute-start.41 = (f32[16,1536]{1,0:T(8,128)S(1)}, f32[16,1536]{1,0:T(8,128)S(1)}, u32[]{:S(2)}, u32[]{:S(2)}) collective-permute-start(f32[16,1536]{1,0:T(8,128)S(1)} %copy-done.50), channel_id=1, source_target_pairs={{0,2},{1,3},{2,4},{3,5},{4,6},{5,7},{6,8},{7,9},{8,10},{9,11},{10,... | collective-permute-start | bytes 294920
  1043.9 18.1 %collective-permute-start.42 = (f32[16,1536]{1,0:T(8,128)S(1)}, f32[16,1536]{1,0:T(8,128)S(1)}, u32[]{:S(2)}, u32[]{:S(2)}) collective-permute-start(f32[16,1536]{1,0:T(8,128)S(1)} %copy-done.50), channel_id=1, source_target_pairs={{0,3},{1,4},{2,5},{3,6},{4,7},{5,8},{6,9},{7,10},{8,11},{9,12},{10... | collective-permute-start | bytes 294920
  1046.8 17.1 %collective-permute-start.43 = (f32[16,1536]{1,0:T(8,128)S(1)}, f32[16,1536]{1,0:T(8,128)S(1)}, u32[]{:S(2)}, u32[]{:S(2)}) collective-permute-start(f32[16,1536]{1,0:T(8,128)S(1)} %copy-done.50), channel_id=1, source_target_pairs={{0,4},{1,5},{2,6},{3,7},{4,8},{5,9},{6,10},{7,11},{8,12},{9,13},{1... | collective-permute-start | bytes 294920
  (217 other events, 2296.2 us)
Sparse Core Ops, SparseCore 0:
  11.6 63.6 all-gather.28
  78.2 53.0 all-gather.30
  134.8 56.6 all-gather.32
  194.8 56.6 all-gather.34
  569.8 97.9 reduce-scatter.16
  726.2 104.7 reduce-scatter.14
